TPU v7x, 32 devices: a whole 2x2x4 slice. The times are simulated.
32 devices in a mesh: section: 4 (over y, x), tok: 4 (over z), head: 2 (over core).
Axes of the slice: x: 2, y: 2, z: 4, core: 2. Of those that a mesh axis runs over, the one named last changes fastest.
Arguments:
- group_in: bfloat16 [4, 512, 2048], P('section', 'tok'), may hold values from -6 to 6
- w_qkv: bfloat16 [4, 3, 2048, 2048], P('section', None, 'tok', 'head'), may hold values from -0.125 to 0.125
- w_out: bfloat16 [4, 2048, 2048], P('section', 'head', 'tok'), may hold values from -0.125 to 0.125
- step_sizes: float32 [4, 512, 4], P('section', 'tok', 'head'), may hold values from 0.05 to 1
- fast_weights: bfloat16 [4, 4, 3, 512, 512], P('section', 'head'), may hold values from -0.25 to 0.25
- momentum: bfloat16 [4, 4, 3, 512, 512], P('section', 'head'), may hold values from -16 to 16
- momentum_decay: float32 [4, 4], P('section', 'head'), may hold values from 0.5 to 0.95
- fast_rate: float32 [4, 4], P('section', 'head'), may hold values from 0.3 to 1
Outputs:
- handed: bfloat16 [4, 512, 2048], P('section', 'tok', 'head')
- fast_next: bfloat16 [4, 4, 3, 512, 512], P('section', 'head')
All inputs are finite; a program needn't handle non-finite values.
Results may differ from a plain program's by a relative error of at most 0.015.
Values may be sent and summed in bfloat16 or wider, within the bound.
A program may use at most 128 MiB of HBM per device.

v0:
```python
import jax
import jax.numpy as jnp
from jax import lax
from jax.sharding import PartitionSpec as P

NS_ITERS = 2
coef_linear = 3.4445
coef_cubic = -4.775
coef_quintic = 2.0315


def passed_along(value, axis, steps):
    count = lax.axis_size(axis)
    pairs = [(source, (source + steps) % count) for source in range(count)]
    return lax.ppermute(value, axis, pairs)


def rms_rows(values_in, epsilon):
    return values_in * lax.rsqrt(jnp.mean(values_in * values_in, axis=-1, keepdims=True) + epsilon)


def fast_grads(key_rows, value_rows, step_rates, weights):
    gate_pre = jnp.einsum(
        "thi,hij->thj", key_rows, weights[:, 0], preferred_element_type=jnp.float32
    )
    up_pre = jnp.einsum("thi,hij->thj", key_rows, weights[:, 1], preferred_element_type=jnp.float32)
    squash = jax.nn.sigmoid(gate_pre)
    hidden = (gate_pre * squash * up_pre).astype(jnp.bfloat16)
    errors = (-(step_rates[:, :, None] * value_rows.astype(jnp.float32))).astype(jnp.bfloat16)
    back_hidden = jnp.einsum(
        "thi,hij->thj", errors, weights[:, 2], preferred_element_type=jnp.float32
    )
    grad_gate = (back_hidden * up_pre * squash * (1.0 + gate_pre * (1.0 - squash))).astype(
        jnp.bfloat16
    )
    grad_up = (back_hidden * gate_pre * squash).astype(jnp.bfloat16)
    grad_first = jnp.einsum("thi,thj->hij", key_rows, grad_gate, preferred_element_type=jnp.float32)
    grad_third = jnp.einsum("thi,thj->hij", key_rows, grad_up, preferred_element_type=jnp.float32)
    grad_second = jnp.einsum("thi,thj->hij", errors, hidden, preferred_element_type=jnp.float32)
    return jnp.stack([grad_first, grad_third, grad_second], axis=1)


def newton_step(rows_in, gathered):
    gram_matrix = jnp.einsum(
        "mij,mik->mjk", gathered, gathered, preferred_element_type=jnp.float32
    ).astype(jnp.bfloat16)
    cubic_term = jnp.einsum(
        "mij,mjk->mik", rows_in, gram_matrix, preferred_element_type=jnp.float32
    )
    quintic_term = jnp.einsum(
        "mij,mjk->mik",
        cubic_term.astype(jnp.bfloat16),
        gram_matrix,
        preferred_element_type=jnp.float32,
    )
    return (
        coef_linear * rows_in.astype(jnp.float32)
        + coef_cubic * cubic_term
        + coef_quintic * quintic_term
    ).astype(jnp.bfloat16)


def apply_fast(queries, updated):
    gate_pre = jnp.einsum(
        "thi,hij->thj", queries, updated[:, 0], preferred_element_type=jnp.float32
    )
    up_pre = jnp.einsum("thi,hij->thj", queries, updated[:, 1], preferred_element_type=jnp.float32)
    hidden = (jax.nn.silu(gate_pre) * up_pre).astype(jnp.bfloat16)
    output = jnp.einsum("thj,hij->thi", hidden, updated[:, 2], preferred_element_type=jnp.float32)
    return rms_rows(output, 1e-05).astype(jnp.bfloat16)


def shards(group_in, w_qkv, w_out, step_sizes, fast_weights, momentum, momentum_decay, fast_rate):
    tokens = group_in[0]
    tok_rows = tokens.shape[0]
    local_heads = fast_weights.shape[1]
    fan_width = fast_weights.shape[3]
    hid_width = fast_weights.shape[4]
    half_width = w_qkv.shape[3]
    projected = jnp.einsum(
        "td,jde->jte",
        tokens,
        lax.all_gather(w_qkv[0], "tok", axis=1, tiled=True),
        preferred_element_type=jnp.float32,
    )
    shaped = projected.reshape(3, tok_rows, local_heads, fan_width)
    queries = rms_rows(shaped[0], 1e-06).astype(jnp.bfloat16)
    key_rows = rms_rows(shaped[1], 1e-06).astype(jnp.bfloat16)
    value_rows = shaped[2].astype(jnp.bfloat16)
    gradients = fast_grads(key_rows, value_rows, step_sizes[0], fast_weights[0])
    decay_rate = momentum_decay[0][:, None, None, None]
    summed = lax.psum(gradients.astype(jnp.bfloat16), "tok").astype(jnp.float32)
    moment = decay_rate * momentum[0].astype(jnp.float32) + summed
    norm_values = jnp.sqrt(jnp.sum(moment * moment, axis=(2, 3), keepdims=True))
    iterate = (moment / (norm_values + 1e-06)).astype(jnp.bfloat16)
    iterate = iterate.reshape(local_heads * 3, fan_width, hid_width)
    for number in range(NS_ITERS):
        iterate = newton_step(iterate, iterate)
    iterate = iterate.reshape(local_heads, 3, fan_width, hid_width)
    updated = (
        fast_weights[0].astype(jnp.float32)
        - fast_rate[0][:, None, None, None] * iterate.astype(jnp.float32)
    ).astype(jnp.bfloat16)
    mixed_heads = apply_fast(queries, updated).reshape(tok_rows, half_width)
    partial_out = jnp.dot(
        mixed_heads,
        lax.all_gather(w_out[0], "tok", axis=1, tiled=True),
        preferred_element_type=jnp.float32,
    )
    summed_out = lax.psum_scatter(
        partial_out.astype(jnp.bfloat16), "head", scatter_dimension=1, tiled=True
    ).astype(jnp.float32)
    share_width = summed_out.shape[1]
    own_tokens = lax.dynamic_slice_in_dim(
        tokens, lax.axis_index("head") * share_width, share_width, 1
    )
    layer_out = (own_tokens.astype(jnp.float32) + summed_out).astype(jnp.bfloat16)
    handed = passed_along(layer_out[None], "section", 1)
    return (handed, updated[None])


def solution(mesh):
    placed = (
        P("section", "tok", None),
        P("section", None, "tok", "head"),
        P("section", "head", "tok"),
        P("section", "tok", "head"),
        P("section", "head", None, None, None),
        P("section", "head", None, None, None),
        P("section", "head"),
        P("section", "head"),
    )
    return jax.shard_map(
        shards,
        mesh=mesh,
        in_specs=placed,
        out_specs=(P("section", "tok", "head"), P("section", "head", None, None, None)),
        check_vma=False,
    )
```

profile of v0, /device:TPU:0, one launch (start us, length us, event | category | flops | bytes accessed | tf_op | source)
XLA Modules:
  0.0 475.3 jit_solution(7633743241635436623)
XLA Ops:
  7.2 4.6 copy.23
  11.9 1.8 copy-done.1
  13.7 1.8 copy.51
  15.6 217.4 %all-gather.5.cloned.1.call-done = bf16[1,3,2048,1024]{2,3,1,0:T(8,128)(2,1)} async-done(((bf16[1,3,512,1024]{2,3,1,0:T(8,128)(2,1)}), bf16[1,3,2048,1024]{2,3,1,0:T(8,128)(2,1)}) %all-gather.5.cloned.1.call-update) | async-done | bytes 12582928 | tf_op jit(solution)/shard_map/all_gather | solution.py:83
  232.9 6.6 %fusion.19 = f32[3,128,1024]{1,2,0:T(8,128)S(1)} fusion(bf16[1,3,2048,1024]{2,3,1,0:T(8,128)(2,1)} %all-gather.5.cloned.1.call-done, bf16[1,128,2048]{2,1,0:T(8,128)(2,1)} %param.8), kind=kOutput, calls=%fused_computation.27 | convolution fusion | flops 1610612736 | bytes 14680064 | tf_op jit(solution)/shard_map/td,jde->jte/dot_general | solution.py:80
  244.2 2.0 pad_maximum_fusion
  247.2 2.0 copy.31
  250.5 115.1 %all-reduce.2.cloned.1.call-done = bf16[2,3,512,512]{3,2,0,1:T(8,128)(2,1)} async-done(((bf16[2,3,512,512]{3,2,0,1:T(8,128)(2,1)}), bf16[2,3,512,512]{3,2,0,1:T(8,128)(2,1)}) %all-reduce.2.cloned.1.call-update) | async-done | bytes 3145744 | tf_op jit(solution)/shard_map/psum | solution.py:92
  365.6 3.5 multiply_reduce_fusion
  369.1 1.3 divide_convert_fusion
  370.6 1.8 convolution_convert_fusion.1
  372.5 1.8 fusion.48
  374.3 2.2 add_convert_fusion.1
  376.5 1.8 convolution_convert_fusion
  378.4 1.8 fusion.49
  380.2 2.5 fusion.7
  382.7 5.4 %fusion.4 = bf16[2,3,512,512]{3,2,0,1:T(8,128)(2,1)S(1)} fusion(f32[2,3,512,512]{3,2,1,0:T(8,128)S(1)} %bitcast.108, f32[2]{0:T(128)S(1)} %bitcast.120, bf16[1,2,3,512,512]{4,3,2,1,0:T(8,128)(2,1)} %param.12), kind=kLoop, calls=%fused_computation.6 | loop fusion | flops 6291456 | bytes 12582920 | tf_op jit(solution)/shard_map/convert_element_type | solution.py:103
  389.2 2.8 multiply_reduce_fusion.1
  393.1 53.9 %all-gather.7.cloned.1.call-done = bf16[1,1024,2048]{2,1,0:T(8,128)(2,1)} async-done(((bf16[1,1024,512]{2,1,0:T(8,128)(2,1)}), bf16[1,1024,2048]{2,1,0:T(8,128)(2,1)}) %all-gather.7.cloned.1.call-update) | async-done | bytes 4194320 | tf_op jit(solution)/shard_map/all_gather | solution.py:107
  447.0 3.9 fusion.16
  450.9 6.6 %reduce-scatter.2.cloned.1.call-done = bf16[128,1024]{1,0:T(8,128)(2,1)} async-done(((bf16[128,2048]{1,0:T(8,128)(2,1)}), bf16[128,1024]{1,0:T(8,128)(2,1)}) %reduce-scatter.2.cloned.1.call-update) | async-done | bytes 262160 | tf_op jit(solution)/shard_map/reduce_scatter | solution.py:110
  458.6 1.7 collective-permute-start
  460.3 5.6 %subtract_convert_fusion = bf16[1,2,3,512,512]{4,3,2,1,0:T(8,128)(2,1)} fusion(f32[1,2,3,512,512]{4,3,2,1,0:T(8,128)} %bitcast.109, bf16[1,2,3,512,512]{4,3,2,1,0:T(8,128)(2,1)S(1)} %copy-done.2, f32[2]{0:T(128)S(1)} %bitcast.121), kind=kLoop, calls=%fused_computation.7 | loop fusion | flops 6291456 | bytes 12582920 | tf_op jit(solution)/shard_map/convert_element_type | solution.py:103
  465.9 2.2 collective-permute-done
  (47 shorter events, 11.2 us)
Async XLA Ops:
  7.2 225.8 %all-gather.5.cloned.1.call-start = ((), (), s32[]{:S(2)}) async-start(), calls=%async_computation.3 | async-start | bytes 15728640 | tf_op jit(solution)/shard_map/all_gather | solution.py:83
  11.8 1.9 copy-start.1
  11.9 353.8 %all-reduce.2.cloned.1.call-start = ((), (), s32[]{:S(2)}) async-start(), calls=%async_computation.1 | async-start | bytes 6291456 | tf_op jit(solution)/shard_map/psum | solution.py:92
  239.5 2.1 copy-start.3
  240.4 1.9 copy-start.9
  246.2 119.4 %copy-start.4 = (bf16[1,2,3,512,512]{4,3,2,1,0:T(8,128)(2,1)S(1)}, bf16[1,2,3,512,512]{4,3,2,1,0:T(8,128)(2,1)}, u32[]{:S(2)}) copy-start(bf16[1,2,3,512,512]{4,3,2,1,0:T(8,128)(2,1)} %param.13) | copy-start | bytes 9437188
  246.2 119.4 %copy-start.8 = (f32[1,2]{1,0:T(1,128)S(1)}, f32[1,2]{1,0:T(1,128)}, u32[]{:S(2)}) copy-start(f32[1,2]{1,0:T(1,128)} %param.14) | copy-start | bytes 28
  246.2 200.7 %all-gather.7.cloned.1.call-start = ((), (), s32[]{:S(2)}) async-start(), calls=%async_computation.4 | async-start | bytes 5242880 | tf_op jit(solution)/shard_map/all_gather | solution.py:107
  247.0 210.5 %reduce-scatter.2.cloned.1.call-start = ((), (), s32[]{:S(2)}) async-start(), calls=%async_computation.2 | async-start | bytes 786432 | tf_op jit(solution)/shard_map/reduce_scatter | solution.py:110
  365.6 3.5 copy-start.5
  380.2 2.5 copy-start.7
  382.7 5.4 %copy-start = (f32[6,512,512]{2,1,0:T(8,128)}, f32[6,512,512]{2,1,0:T(8,128)S(1)}, u32[]{:S(2)}) copy-start(f32[6,512,512]{2,1,0:T(8,128)S(1)} %fusion.7) | copy-start | bytes 18874372
  382.7 5.4 %copy-start.6 = (f32[128,2,512]{2,0,1:T(8,128)S(1)}, f32[128,2,512]{2,0,1:T(8,128)}, u32[]{:S(2)}) copy-start(f32[128,2,512]{2,0,1:T(8,128)} %copy.31) | copy-start | bytes 1572868
  447.0 13.3 %copy-start.2 = (bf16[1,2,3,512,512]{4,3,2,1,0:T(8,128)(2,1)S(1)}, bf16[1,2,3,512,512]{4,3,2,1,0:T(8,128)(2,1)}, u32[]{:S(2)}) copy-start(bf16[1,2,3,512,512]{4,3,2,1,0:T(8,128)(2,1)} %param.12) | copy-start | bytes 9437188
  458.6 9.5 %collective-permute-start = (bf16[1,128,1024]{2,1,0:T(8,128)(2,1)S(1)}, bf16[1,128,1024]{2,1,0:T(8,128)(2,1)S(1)}, u32[]{:S(2)}, u32[]{:S(2)}) collective-permute-start(bf16[1,128,1024]{2,1,0:T(8,128)(2,1)S(1)} %fusion.36), channel_id=1, source_target_pairs={{0,8},{8,16},{16,24},{24,0},{1,9},{9,17},{17,25},{25,1},{2,10},{10... | collective-permute-start | bytes 786440 | tf_op jit(solution)/shard_map/ppermute | solution.py:15
Sparse Core Ops, SparseCore 0:
  12.0 220.8 all-gather.4
  246.4 119.2 all-reduce.1
  367.2 79.7 all-gather.6
  451.0 6.3 reduce-scatter.1
where the time goes:
time: 476 us; the launch traced here: 475 us
  waiting for transfers between devices  396 us (83%)
  matrix products  28.9 us (6%)
  other arithmetic  21.3 us (4%)
  between operations  14 us (3%)
  local copies, waits for them, and re-layouts  13.2 us (3%)
    all_gather x1, waiting for transfers between devices, shards(): lax.all_gather(w_qkv[0], 'tok', axis=1, tiled=True)  217 us
    psum x1, waiting for transfers between devices, shards(): summed = lax.psum(gradients.astype(jnp.bfloat16), 'tok').astype(jnp.float32)  115 us
    all_gather x1, waiting for transfers between devices, shards(): lax.all_gather(w_out[0], 'tok', axis=1, tiled=True)  53.9 us
    convert_element_type x2, other arithmetic, shards(): updated = (fast_weights[0].astype(jnp.float32) - fast_rate[0][:, None, No...  10.9 us
    unnamed x23, local copies, waits for them, and re-layouts  10.1 us
  transfers between devices with their start and end apart: 5, of which 5 were waited for; matrix products, arithmetic and copies ran while one was open for 8% of the time, Pallas kernels for 0%

commit v1 on v0

--- a/solution.py
+++ b/solution.py
@@ -104,7 +104,7 @@
     mixed_heads = apply_fast(queries, updated).reshape(tok_rows, half_width)
     partial_out = jnp.dot(
         mixed_heads,
-        lax.all_gather(w_out[0], "tok", axis=1, tiled=True),
+        jnp.concatenate(lax.all_gather(w_out[0], "tok"), axis=1),
         preferred_element_type=jnp.float32,
     )
     summed_out = lax.psum_scatter(

time: 476 us -> 494 us (1.038)
  waiting for transfers between devices: 396 us -> 407 us
  local copies, waits for them, and re-layouts: 13.2 us -> 19.2 us
    all_gather x1, waiting for transfers between devices: 53.9 us -> 66.9 us  [shards(): lax.all_gather(w_out[0], 'tok')]
    all_gather x0 -> x1, local copies, waits for them, and re-layouts: none -> 6.28 us  [shards(): lax.all_gather(w_out[0], 'tok')]
  transfers between devices with their start and end apart: 5 -> 5, of which waited for: 5 -> 5; matrix products, arithmetic and copies ran while one was open for 8% -> 6% of each run, Pallas kernels for 0% -> 0%
where the time goes in v1:
time: 494 us; the launch traced here: 493 us
  waiting for transfers between devices  407 us (82%)
  matrix products  29.7 us (6%)
  other arithmetic  21.2 us (4%)
  local copies, waits for them, and re-layouts  19.2 us (4%)
  between operations  14 us (3%)
    all_gather x1, waiting for transfers between devices, shards(): lax.all_gather(w_qkv[0], 'tok', axis=1, tiled=True)  217 us
    psum x1, waiting for transfers between devices, shards(): summed = lax.psum(gradients.astype(jnp.bfloat16), 'tok').astype(jnp.float32)  113 us
    all_gather x1, waiting for transfers between devices, shards(): lax.all_gather(w_out[0], 'tok')  66.9 us
    convert_element_type x2, other arithmetic, shards(): updated = (fast_weights[0].astype(jnp.float32) - fast_rate[0][:, None, No...  10.9 us
  transfers between devices with their start and end apart: 5, of which 5 were waited for; matrix products, arithmetic and copies ran while one was open for 6% of the time, Pallas kernels for 0%

profile of v1, /device:TPU:0, one launch (start us, length us, event | category | flops | bytes accessed | tf_op | source)
XLA Modules:
  0.0 493.1 jit_solution(15038829600062195262)
XLA Ops:
  7.2 4.6 copy.37
  13.7 1.8 copy.70
  15.6 217.4 %all-gather.6.cloned.1.call-done = bf16[1,3,2048,1024]{2,3,1,0:T(8,128)(2,1)} async-done(((bf16[1,3,512,1024]{2,3,1,0:T(8,128)(2,1)}), bf16[1,3,2048,1024]{2,3,1,0:T(8,128)(2,1)}) %all-gather.6.cloned.1.call-update) | async-done | bytes 12582928 | tf_op jit(solution)/shard_map/all_gather | solution.py:83
  232.9 6.6 %fusion.14 = f32[3,128,1024]{1,2,0:T(8,128)S(1)} fusion(bf16[1,3,2048,1024]{2,3,1,0:T(8,128)(2,1)} %all-gather.6.cloned.1.call-done, bf16[1,128,2048]{2,1,0:T(8,128)(2,1)} %param.8), kind=kOutput, calls=%fused_computation.25 | convolution fusion | flops 1610612736 | bytes 14680064 | tf_op jit(solution)/shard_map/td,jde->jte/dot_general | solution.py:80
  244.5 2.0 pad_maximum_fusion
  246.6 66.9 %all-gather.4.cloned.1.call-done = bf16[4,1024,512]{2,1,0:T(8,128)(2,1)} async-done(((bf16[1,1024,512]{2,1,0:T(8,128)(2,1)}), bf16[4,1024,512]{2,1,0:T(8,128)(2,1)}) %all-gather.4.cloned.1.call-update) | async-done | bytes 4194320 | tf_op jit(solution)/shard_map/all_gather | solution.py:107
  313.5 6.3 %copy.50 = bf16[4,1024,512]{1,2,0:T(8,128)(2,1)} copy(bf16[4,1024,512]{2,1,0:T(8,128)(2,1)} %all-gather.4.cloned.1.call-done) | data formatting | bytes 8388608 | tf_op jit(solution)/shard_map/all_gather | solution.py:107
  319.7 2.2 copy.45
  323.1 112.9 %all-reduce.2.cloned.1.call-done = bf16[2,3,512,512]{3,2,0,1:T(8,128)(2,1)} async-done(((bf16[2,3,512,512]{3,2,0,1:T(8,128)(2,1)}), bf16[2,3,512,512]{3,2,0,1:T(8,128)(2,1)}) %all-reduce.2.cloned.1.call-update) | async-done | bytes 3145744 | tf_op jit(solution)/shard_map/psum | solution.py:92
  436.0 3.5 multiply_reduce_fusion
  439.5 1.3 divide_convert_fusion
  441.0 1.8 convolution_convert_fusion.2
  442.8 1.8 fusion.43
  444.6 2.2 add_convert_fusion.1
  446.9 1.8 convolution_convert_fusion.1
  448.7 1.8 fusion.44
  450.5 2.5 fusion.5
  453.1 5.4 %fusion.4 = bf16[2,3,512,512]{3,2,0,1:T(8,128)(2,1)S(1)} fusion(f32[2,3,512,512]{3,2,1,0:T(8,128)S(1)} %bitcast.107, f32[2]{0:T(128)S(1)} %bitcast.120, bf16[1,2,3,512,512]{4,3,2,1,0:T(8,128)(2,1)} %param.12), kind=kLoop, calls=%fused_computation.6 | loop fusion | flops 6291456 | bytes 12582920 | tf_op jit(solution)/shard_map/convert_element_type | solution.py:103
  459.6 2.8 multiply_reduce_fusion.1
  463.5 4.7 convolution_convert_fusion
  468.2 7.1 %reduce-scatter.2.cloned.1.call-done = bf16[128,1024]{1,0:T(8,128)(2,1)} async-done(((bf16[128,2048]{1,0:T(8,128)(2,1)}), bf16[128,1024]{1,0:T(8,128)(2,1)}) %reduce-scatter.2.cloned.1.call-update) | async-done | bytes 262160 | tf_op jit(solution)/shard_map/reduce_scatter | solution.py:110
  476.4 1.7 collective-permute-start
  478.1 5.6 %subtract_convert_fusion = bf16[1,2,3,512,512]{4,3,2,1,0:T(8,128)(2,1)} fusion(f32[1,2,3,512,512]{4,3,2,1,0:T(8,128)} %bitcast.108, bf16[1,2,3,512,512]{4,3,2,1,0:T(8,128)(2,1)S(1)} %copy-done.2, f32[2]{0:T(128)S(1)} %bitcast.121), kind=kLoop, calls=%fused_computation.7 | loop fusion | flops 6291456 | bytes 12582920 | tf_op jit(solution)/shard_map/convert_element_type | solution.py:103
  483.7 2.2 collective-permute-done
  (48 shorter events, 12.3 us)
Async XLA Ops:
  7.2 225.8 %all-gather.6.cloned.1.call-start = ((), (), s32[]{:S(2)}) async-start(), calls=%async_computation.4 | async-start | bytes 15728640 | tf_op jit(solution)/shard_map/all_gather | solution.py:83
  11.8 1.9 copy-start.1
  11.9 301.6 %all-gather.4.cloned.1.call-start = ((), (), s32[]{:S(2)}) async-start(), calls=%async_computation.2 | async-start | bytes 5242880 | tf_op jit(solution)/shard_map/all_gather | solution.py:107
  12.6 423.4 %all-reduce.2.cloned.1.call-start = ((), (), s32[]{:S(2)}) async-start(), calls=%async_computation.1 | async-start | bytes 6291456 | tf_op jit(solution)/shard_map/psum | solution.py:92
  239.5 2.4 copy-start.3
  239.5 2.7 copy-start.9
  246.5 189.5 %copy-start.4 = (bf16[1,2,3,512,512]{4,3,2,1,0:T(8,128)(2,1)S(1)}, bf16[1,2,3,512,512]{4,3,2,1,0:T(8,128)(2,1)}, u32[]{:S(2)}) copy-start(bf16[1,2,3,512,512]{4,3,2,1,0:T(8,128)(2,1)} %param.13) | copy-start | bytes 9437188
  246.5 189.5 %copy-start.8 = (f32[1,2]{1,0:T(1,128)S(1)}, f32[1,2]{1,0:T(1,128)}, u32[]{:S(2)}) copy-start(f32[1,2]{1,0:T(1,128)} %param.14) | copy-start | bytes 28
  246.5 228.8 %reduce-scatter.2.cloned.1.call-start = ((), (), s32[]{:S(2)}) async-start(), calls=%async_computation.3 | async-start | bytes 786432 | tf_op jit(solution)/shard_map/reduce_scatter | solution.py:110
  436.0 3.5 copy-start.5
  450.5 2.5 copy-start.7
  453.0 5.4 %copy-start = (f32[6,512,512]{2,1,0:T(8,128)}, f32[6,512,512]{2,1,0:T(8,128)S(1)}, u32[]{:S(2)}) copy-start(f32[6,512,512]{2,1,0:T(8,128)S(1)} %fusion.5) | copy-start | bytes 18874372
  453.1 5.4 %copy-start.6 = (f32[128,2,512]{2,0,1:T(8,128)S(1)}, f32[128,2,512]{2,0,1:T(8,128)}, u32[]{:S(2)}) copy-start(f32[128,2,512]{2,0,1:T(8,128)} %copy.45) | copy-start | bytes 1572868
  463.5 14.6 %copy-start.2 = (bf16[1,2,3,512,512]{4,3,2,1,0:T(8,128)(2,1)S(1)}, bf16[1,2,3,512,512]{4,3,2,1,0:T(8,128)(2,1)}, u32[]{:S(2)}) copy-start(bf16[1,2,3,512,512]{4,3,2,1,0:T(8,128)(2,1)} %param.12) | copy-start | bytes 9437188
  476.4 9.4 %collective-permute-start = (bf16[1,128,1024]{2,1,0:T(8,128)(2,1)S(1)}, bf16[1,128,1024]{2,1,0:T(8,128)(2,1)S(1)}, u32[]{:S(2)}, u32[]{:S(2)}) collective-permute-start(bf16[1,128,1024]{2,1,0:T(8,128)(2,1)S(1)} %fusion.31), channel_id=1, source_target_pairs={{0,8},{8,16},{16,24},{24,0},{1,9},{9,17},{17,25},{25,1},{2,10},{10... | collective-permute-start | bytes 786440 | tf_op jit(solution)/shard_map/ppermute | solution.py:15
Sparse Core Ops, SparseCore 0:
  12.0 220.8 all-gather.5
  234.5 78.9 all-gather.3
  316.4 119.5 all-reduce.1
  468.3 6.9 reduce-scatter.1
